TPU v7x, 32 devices: a whole 2x2x4 slice. The times are simulated.
32 devices in a mesh: blk: 8 (over z, core), uly: 4 (over y, x).
Axes of the slice: x: 2, y: 2, z: 4, core: 2. Of those that a mesh axis runs over, the one named last changes fastest.
Arguments:
- queries: bfloat16 [1024, 128, 128], P(('blk', 'uly')), may hold values from -8 to 8
- query_tangents: bfloat16 [1024, 128, 4, 128], P(('blk', 'uly')), may hold values from -6 to 6
- keys: bfloat16 [1024, 8, 128], P(('blk', 'uly')), may hold values from -8 to 8
- key_tangents: bfloat16 [1024, 8, 4, 128], P(('blk', 'uly')), may hold values from -6 to 6
- values: bfloat16 [1024, 8, 128], P(('blk', 'uly')), may hold values from -6 to 6
- value_tangents: bfloat16 [1024, 8, 4, 128], P(('blk', 'uly')), may hold values from -6 to 6
- span_order: int32 [16], replicated, may hold values from 0 to 15, as said below
Outputs:
- attention_out: bfloat16 [1024, 128, 128], P(('blk', 'uly'))
- tangent_out: bfloat16 [1024, 128, 4, 128], P(('blk', 'uly'))
Inputs may be any that keep to these rules, and one draw needn't show every extreme that they name: span_order is a permutation of the span positions; for every b the stored spans 2 * b and 2 * b + 1 hold positions c and 15 - c for some c.
All inputs are finite; a program needn't handle non-finite values.
Results may differ from a plain program's by a relative error of at most 0.0055.
Values may be sent and summed in bfloat16 or wider, within the bound.
A program may use at most 128 MiB of HBM per device.

v0:
```python
import jax
import jax.numpy as jnp
from jax import lax
from jax.sharding import PartitionSpec as P

HQ = 128
KVH = 8


def positions(stored, span_order, span_rows):
    span_ids = stored // span_rows
    table_ids = jnp.arange(span_order.shape[0], dtype=jnp.int32)
    looked_up = jnp.sum(
        jnp.where(span_ids[:, None] == table_ids[None, :], span_order[None, :], 0), axis=1
    )
    return looked_up * span_rows + stored % span_rows


def per_device(queries, query_tangents, keys, key_tangents, values, value_tangents, span_order):
    local_queries, local_tangents = (
        lax.all_to_all(queries, "uly", split_axis=1, concat_axis=0, tiled=True),
        lax.all_to_all(query_tangents, "uly", split_axis=1, concat_axis=0, tiled=True),
    )
    query_rows = local_queries.shape[0]
    span_rows = query_rows // 2
    head_size = local_queries.shape[2]
    group = HQ // KVH
    kv_local = local_queries.shape[1] // group
    probes = local_tangents.shape[2]
    scaling = head_size ** (-0.5)
    stored = lax.axis_index("blk") * query_rows + jnp.arange(query_rows, dtype=jnp.int32)
    query_places = positions(stored, span_order, span_rows)
    latest = jnp.max(query_places)
    query_heads = jnp.transpose(
        local_queries.reshape(query_rows, kv_local, group, head_size), (1, 2, 0, 3)
    )
    tangent_heads = jnp.transpose(
        local_tangents.reshape(query_rows, kv_local, group, probes, head_size), (1, 2, 3, 0, 4)
    )

    def update(carry, block):
        key_block, key_tan, value_block, value_tan, key_places = block
        running_max, totals, primal_sums, tangent_sums, shifts = carry
        visible = key_places[None, :] <= query_places[:, None]
        scores = (
            jnp.einsum("grqd,kgd->grqk", query_heads, key_block, preferred_element_type=jnp.float32)
            * scaling
        )
        scores = jnp.where(visible[None, None], scores, -1e30)
        new_max = jnp.maximum(running_max, jnp.max(scores, axis=-1))
        rescale = jnp.exp(running_max - new_max)
        weights_full = jnp.where(visible[None, None], jnp.exp(scores - new_max[..., None]), 0.0)
        weights_half = weights_full.astype(jnp.bfloat16)
        score_tan = jnp.einsum(
            "grpqd,kgd->grpqk", tangent_heads, key_block, preferred_element_type=jnp.float32
        )
        score_tan = score_tan + jnp.einsum(
            "grqd,kgpd->grpqk", query_heads, key_tan, preferred_element_type=jnp.float32
        )
        weighted = weights_full[:, :, None] * (score_tan * scaling)
        totals = totals * rescale + jnp.sum(weights_full, axis=-1)
        primal_sums = primal_sums * rescale[..., None] + jnp.einsum(
            "grqk,kgd->grqd", weights_half, value_block, preferred_element_type=jnp.float32
        )
        shifts = shifts * rescale[:, :, None] + jnp.sum(weighted, axis=-1)
        tangent_sums = tangent_sums * rescale[:, :, None, :, None]
        tangent_sums = tangent_sums + jnp.einsum(
            "grpqk,kgd->grpqd",
            weighted.astype(jnp.bfloat16),
            value_block,
            preferred_element_type=jnp.float32,
        )
        tangent_sums = tangent_sums + jnp.einsum(
            "grqk,kgpd->grpqd", weights_half, value_tan, preferred_element_type=jnp.float32
        )
        return (new_max, totals, primal_sums, tangent_sums, shifts)

    def keep_state(carry, block):
        return carry

    def visit(carry, block):
        reachable = jnp.min(block[4]) <= latest
        return (lax.cond(reachable, update, keep_state, carry, block), None)

    initial = (
        jnp.full((kv_local, group, query_rows), -1e30, jnp.float32),
        jnp.zeros((kv_local, group, query_rows), jnp.float32),
        jnp.zeros((kv_local, group, query_rows, head_size), jnp.float32),
        jnp.zeros((kv_local, group, probes, query_rows, head_size), jnp.float32),
        jnp.zeros((kv_local, group, probes, query_rows), jnp.float32),
    )
    head_keys, head_key_tan, head_values, head_value_tan = (
        lax.all_to_all(keys, "uly", split_axis=1, concat_axis=0, tiled=True),
        lax.all_to_all(key_tangents, "uly", split_axis=1, concat_axis=0, tiled=True),
        lax.all_to_all(values, "uly", split_axis=1, concat_axis=0, tiled=True),
        lax.all_to_all(value_tangents, "uly", split_axis=1, concat_axis=0, tiled=True),
    )
    carry = initial
    key_piece = lax.all_gather(head_keys, "blk", axis=0, tiled=True)
    key_tan_piece = lax.all_gather(head_key_tan, "blk", axis=0, tiled=True)
    value_piece = lax.all_gather(head_values, "blk", axis=0, tiled=True)
    value_tan_piece = lax.all_gather(head_value_tan, "blk", axis=0, tiled=True)
    piece_rows = key_piece.shape[0]
    block_rows = 256
    block_total = piece_rows // block_rows
    places = positions(jnp.arange(piece_rows, dtype=jnp.int32), span_order, span_rows)
    stacked = (
        key_piece.reshape(block_total, block_rows, kv_local, head_size),
        key_tan_piece.reshape(block_total, block_rows, kv_local, probes, head_size),
        value_piece.reshape(block_total, block_rows, kv_local, head_size),
        value_tan_piece.reshape(block_total, block_rows, kv_local, probes, head_size),
        places.reshape(block_total, block_rows),
    )
    carry, unused = lax.scan(visit, carry, stacked)
    running_max, totals, primal_sums, tangent_sums, shifts = carry
    primal = primal_sums / totals[..., None]
    tangent = (
        tangent_sums / totals[:, :, None, :, None]
        - primal[:, :, None] * (shifts / totals[:, :, None])[..., None]
    )
    output_rows = jnp.transpose(primal.astype(jnp.bfloat16), (2, 0, 1, 3)).reshape(
        query_rows, kv_local * group, head_size
    )
    tangent_rows = jnp.transpose(tangent.astype(jnp.bfloat16), (3, 0, 1, 2, 4)).reshape(
        query_rows, kv_local * group, probes, head_size
    )
    attention_out, tangent_out = (
        lax.all_to_all(output_rows, "uly", split_axis=0, concat_axis=1, tiled=True),
        lax.all_to_all(tangent_rows, "uly", split_axis=0, concat_axis=1, tiled=True),
    )
    return (attention_out, tangent_out)


def solution(mesh):
    placed = (
        P(("blk", "uly"), None, None),
        P(("blk", "uly"), None, None, None),
        P(("blk", "uly"), None, None),
        P(("blk", "uly"), None, None, None),
        P(("blk", "uly"), None, None),
        P(("blk", "uly"), None, None, None),
        P(),
    )
    return jax.shard_map(
        per_device,
        mesh=mesh,
        in_specs=placed,
        out_specs=(P(("blk", "uly"), None, None), P(("blk", "uly"), None, None, None)),
        check_vma=False,
    )
```

profile of v0, /device:TPU:10, one launch (start us, length us, event | category | flops | bytes accessed | tf_op | source)
XLA Modules:
  0.0 421.9 jit_solution(10656126634466372391)
XLA Ops:
  8.3 8.7 %all_to_all.138 = bf16[32,8,4,128]{3,0,2,1:T(8,128)(2,1)S(1)} all-to-all(bf16[32,8,4,128]{3,0,2,1:T(8,128)(2,1)S(1)} %copy.84), channel_id=1, replica_groups=mesh['blk'=8,'uly'=4] {'uly'}, dimensions={1} | all-to-all | bytes 524288 | tf_op jit(solution)/shard_map/all_to_all | solution.py:94
  19.2 4.4 %all-to-all-start = ((bf16[32,8,128]{2,0,1:T(8,128)(2,1)}), bf16[32,8,128]{2,0,1:T(8,128)(2,1)S(1)}, u32[]{:S(2)}, u32[]{:S(2)}) async-start(bf16[32,8,128]{2,0,1:T(8,128)(2,1)} %copy.76), calls=%async_computation | async-start | bytes 131072 | tf_op jit(solution)/shard_map/all_to_all | solution.py:93
  25.0 2.1 all-to-all-done
  27.1 4.5 %all-to-all-start.2 = ((bf16[32,8,128]{2,0,1:T(8,128)(2,1)}), bf16[32,8,128]{2,0,1:T(8,128)(2,1)S(1)}, u32[]{:S(2)}, u32[]{:S(2)}) async-start(bf16[32,8,128]{2,0,1:T(8,128)(2,1)} %copy.80), calls=%async_computation.2 | async-start | bytes 131072 | tf_op jit(solution)/shard_map/all_to_all | solution.py:95
  31.7 1.8 copy.86
  33.4 1.8 all-to-all-done.2
  35.2 4.7 %all-to-all-start.5 = ((bf16[32,8,4,128]{3,0,2,1:T(8,128)(2,1)}), bf16[32,8,4,128]{3,0,2,1:T(8,128)(2,1)S(1)}, u32[]{:S(2)}, u32[]{:S(2)}) async-start(bf16[32,8,4,128]{3,0,2,1:T(8,128)(2,1)} %copy.86), calls=%async_computation.5 | async-start | bytes 524288 | tf_op jit(solution)/shard_map/all_to_all | solution.py:96
  39.9 2.9 copy.78
  42.8 1.7 all-to-all-done.5
  44.5 4.2 %all-to-all-start.1 = ((bf16[32,128,128]{2,0,1:T(8,128)(2,1)}), bf16[32,128,128]{2,0,1:T(8,128)(2,1)S(1)}, u32[]{:S(2)}, u32[]{:S(2)}) async-start(bf16[32,128,128]{2,0,1:T(8,128)(2,1)} %copy.78), calls=%async_computation.1 | async-start | bytes 2097152 | tf_op jit(solution)/shard_map/all_to_all | solution.py:21
  49.5 6.6 %copy.82 = bf16[32,128,4,128]{3,2,0,1:T(4,128)(2,1)} copy(bf16[32,128,4,128]{3,2,1,0:T(4,128)(2,1)} %param.12) | data formatting | bytes 8388608 | tf_op args[1]
  56.1 1.6 all-to-all-done.1
  57.7 5.5 %all-to-all-start.3 = ((bf16[32,128,4,128]{3,2,0,1:T(4,128)(2,1)}), bf16[32,128,4,128]{3,2,0,1:T(4,128)(2,1)}, u32[]{:S(2)}, u32[]{:S(2)}) async-start(bf16[32,128,4,128]{3,2,0,1:T(4,128)(2,1)} %copy.82), calls=%async_computation.3 | async-start | bytes 8388608 | tf_op jit(solution)/shard_map/all_to_all | solution.py:22
  64.1 17.9 %all_gather.12 = bf16[1024,2,128]{2,0,1:T(8,128)(2,1)S(1)} all-gather(bf16[128,2,128]{2,0,1:T(8,128)(2,1)S(1)} %bitcast.140), channel_id=1, replica_groups=mesh['blk'=8,'uly'=4] {'blk'}, dimensions={0}, use_global_device_ids=true | all-gather | bytes 589824 | tf_op jit(solution)/shard_map/all_gather | solution.py:99
  82.8 15.1 %all_gather.13 = bf16[1024,2,128]{2,0,1:T(8,128)(2,1)S(1)} all-gather(bf16[128,2,128]{2,0,1:T(8,128)(2,1)S(1)} %bitcast.141), channel_id=1, replica_groups=mesh['blk'=8,'uly'=4] {'blk'}, dimensions={0}, use_global_device_ids=true | all-gather | bytes 589824 | tf_op jit(solution)/shard_map/all_gather | solution.py:101
  98.9 6.1 %all-to-all-done.3 = bf16[32,128,4,128]{3,2,0,1:T(4,128)(2,1)} async-done(((bf16[32,128,4,128]{3,2,0,1:T(4,128)(2,1)}), bf16[32,128,4,128]{3,2,0,1:T(4,128)(2,1)}, u32[]{:S(2)}, u32[]{:S(2)}) %all-to-all-start.3) | async-done | bytes 4194336 | tf_op jit(solution)/shard_map/all_to_all | solution.py:22
  105.0 5.4 %copy.83 = bf16[4,32,32,4,128]{4,1,0,3,2:T(8,128)(2,1)} copy(bf16[4,32,32,4,128]{4,3,1,2,0:T(4,128)(2,1)} %bitcast.37) | data formatting | bytes 8388608 | tf_op jit(solution)/shard_map/all_to_all | solution.py:22
  110.4 3.1 copy.90
  113.5 1.7 copy.91
  115.3 4.3 %broadcast_in_dim.87 = f32[2,16,4,128,128]{4,3,2,1,0:T(8,128)} broadcast(f32[]{:T(128)} %constant.103.clone.1), dimensions={} | broadcast | bytes 8388612 | tf_op jit(solution)/shard_map/broadcast_in_dim | solution.py:89
  119.5 1.6 broadcast_in_dim.86
  121.1 212.6 %while.18 = (s32[]{:T(128)}, f32[2,16,128]{2,1,0:T(8,128)S(1)}, f32[2,16,128]{2,1,0:T(8,128)S(1)}, f32[2,16,128,128]{3,2,1,0:T(8,128)}, f32[2,16,4,128,128]{4,3,...) while((s32[]{:T(128)}, f32[2,16,128]{2,1,0:T(8,128)S(1)}, ...), condition=%wide.region_10.11_spmd, body=%wide.region_3.10_spmd.sunk | while | flops 4875936256 | bytes 138631600 | solution.py:114
  123.3 51.1 %conditional.2 = ((f32[2,16,128]{2,1,0:T(8,128)S(1)}, f32[2,16,128]{2,1,0:T(8,128)S(1)}, f32[2,16,128,128]{3,2,1,0:T(8,128)}, f32[2,16,4,128,128]{4,3,2,1,0:T(8,128)}, f32[2,16,4,128]{3,2,1,0:T(4,128)S(1)})) conditional(s32[]{:T(128)} %convert_element_type.33, (f32[2,16,128]{2,1,0:T(8,128)S(1)}, f32[2,16,128]{2,1,0:T(8,128)S(1)}, ...), branch_computations={%region_5.5_spmd, %region_6.9_spmd} | conditional | flops 4875935744 | bytes 138629216 | solution.py:83
  123.4 1.6 fusion.3
  125.1 3.3 broadcast_multiply_fusion
  128.4 9.1 %fusion.7 = f32[2,256,4,16,128]{4,1,2,3,0:T(8,128)} fusion(bf16[2,16,128,128]{3,2,1,0:T(8,128)(2,1)S(1)} %get-tuple-element.183, bf16[4,256,2,4,128]{4,1,3,2,0:T(8,128)(2,1)} %get-tuple-element.189, s32[]{:T(128)} %get-tuple-element.182), kind=kOutput, calls=%fused_computation.13 | convolution fusion | flops 1073741824 | bytes 18350592 | tf_op jit(solution)/shard_map/while/body/eval_jaxpr/cond/branch_1_fun/grqd,kgpd->grpqk/dot_general | solution.py:57
  137.5 13.2 %fusion.40 = (f32[2,16,4,128]{3,2,1,0:T(4,128)S(1)}, bf16[2,16,4,128,256]{3,4,2,1,0:T(8,128)(2,1)}) fusion(f32[2,16,128,256]{2,3,1,0:T(8,128)} %get-tuple-element.327, f32[2,256,4,16,128]{4,1,2,3,0:T(8,128)} %fusion.7, bf16[2,16,4,128,128]{4,3,2,1,0:T(8,128)(2,1)} %get-tuple-element.188, bf16[4,256,2,128]{3,1,2,0:T(8,128)(2,1)} %get-tuple-element.181, ...), kind=kOutput, calls=%fused_computation.70 | convolution fusion | flops 1090502656 | bytes 33751552 | tf_op jit(solution)/shard_map/while/body/eval_jaxpr/cond/branch_1_fun/grpqd,kgd->grpqk/dot_general | solution.py:54
  150.8 10.0 %fusion.1 = f32[2,16,4,128,128]{4,3,2,1,0:T(8,128)} fusion(bf16[2,16,4,128,256]{3,4,2,1,0:T(8,128)(2,1)} %get-tuple-element.332, bf16[4,256,2,128]{3,1,2,0:T(8,128)(2,1)} %get-tuple-element.186, s32[]{:T(128)} %get-tuple-element.182), kind=kOutput, calls=%fused_computation.3 | convolution fusion | flops 1073741824 | bytes 16908800 | tf_op jit(solution)/shard_map/while/body/eval_jaxpr/cond/branch_1_fun/grpqk,kgd->grpqd/dot_general | solution.py:67
  160.8 9.5 %bitcast_add_fusion.1 = f32[2,16,4,128,128]{4,3,2,1,0:T(8,128)} fusion(f32[2,16,4,128,128]{4,3,2,1,0:T(8,128)} %fusion.1, f32[2,16,4,128,128]{4,3,2,1,0:T(8,128)} %get-tuple-element.187, f32[2,16,128]{2,1,0:T(8,128)S(1)} %get-tuple-element.320, bf16[4,256,2,4,128]{4,1,3,2,0:T(8,128)(2,1)S(1)} %get-tuple-element.190, s32[]{:T(128)} %get-tuple-element.182, ...), kind=kOutput, calls=%fused_computation.2 | convolution fusion | flops 1085276160 | bytes 29949956 | tf_op jit(solution)/shard_map/while/body/eval_jaxpr/cond/branch_1_fun/grqk,kgpd->grpqd/dot_general | solution.py:73
  170.4 2.7 multiply_add_fusion
  176.4 51.1 %conditional.2 = ((f32[2,16,128]{2,1,0:T(8,128)S(1)}, f32[2,16,128]{2,1,0:T(8,128)S(1)}, f32[2,16,128,128]{3,2,1,0:T(8,128)}, f32[2,16,4,128,128]{4,3,2,1,0:T(8,128)}, f32[2,16,4,128]{3,2,1,0:T(4,128)S(1)})) conditional(s32[]{:T(128)} %convert_element_type.33, (f32[2,16,128]{2,1,0:T(8,128)S(1)}, f32[2,16,128]{2,1,0:T(8,128)S(1)}, ...), branch_computations={%region_5.5_spmd, %region_6.9_spmd} | conditional | flops 4875935744 | bytes 138629216 | solution.py:83
  176.5 1.6 fusion.3
  178.2 3.3 broadcast_multiply_fusion
  181.5 9.1 %fusion.7 = f32[2,256,4,16,128]{4,1,2,3,0:T(8,128)} fusion(bf16[2,16,128,128]{3,2,1,0:T(8,128)(2,1)S(1)} %get-tuple-element.183, bf16[4,256,2,4,128]{4,1,3,2,0:T(8,128)(2,1)} %get-tuple-element.189, s32[]{:T(128)} %get-tuple-element.182), kind=kOutput, calls=%fused_computation.13 | convolution fusion | flops 1073741824 | bytes 18350592 | tf_op jit(solution)/shard_map/while/body/eval_jaxpr/cond/branch_1_fun/grqd,kgpd->grpqk/dot_general | solution.py:57
  190.6 13.2 %fusion.40 = (f32[2,16,4,128]{3,2,1,0:T(4,128)S(1)}, bf16[2,16,4,128,256]{3,4,2,1,0:T(8,128)(2,1)}) fusion(f32[2,16,128,256]{2,3,1,0:T(8,128)} %get-tuple-element.327, f32[2,256,4,16,128]{4,1,2,3,0:T(8,128)} %fusion.7, bf16[2,16,4,128,128]{4,3,2,1,0:T(8,128)(2,1)} %get-tuple-element.188, bf16[4,256,2,128]{3,1,2,0:T(8,128)(2,1)} %get-tuple-element.181, ...), kind=kOutput, calls=%fused_computation.70 | convolution fusion | flops 1090502656 | bytes 33751552 | tf_op jit(solution)/shard_map/while/body/eval_jaxpr/cond/branch_1_fun/grpqd,kgd->grpqk/dot_general | solution.py:54
  203.9 10.0 %fusion.1 = f32[2,16,4,128,128]{4,3,2,1,0:T(8,128)} fusion(bf16[2,16,4,128,256]{3,4,2,1,0:T(8,128)(2,1)} %get-tuple-element.332, bf16[4,256,2,128]{3,1,2,0:T(8,128)(2,1)} %get-tuple-element.186, s32[]{:T(128)} %get-tuple-element.182), kind=kOutput, calls=%fused_computation.3 | convolution fusion | flops 1073741824 | bytes 16908800 | tf_op jit(solution)/shard_map/while/body/eval_jaxpr/cond/branch_1_fun/grpqk,kgd->grpqd/dot_general | solution.py:67
  213.9 9.5 %bitcast_add_fusion.1 = f32[2,16,4,128,128]{4,3,2,1,0:T(8,128)} fusion(f32[2,16,4,128,128]{4,3,2,1,0:T(8,128)} %fusion.1, f32[2,16,4,128,128]{4,3,2,1,0:T(8,128)} %get-tuple-element.187, f32[2,16,128]{2,1,0:T(8,128)S(1)} %get-tuple-element.320, bf16[4,256,2,4,128]{4,1,3,2,0:T(8,128)(2,1)S(1)} %get-tuple-element.190, s32[]{:T(128)} %get-tuple-element.182, ...), kind=kOutput, calls=%fused_computation.2 | convolution fusion | flops 1085276160 | bytes 29949956 | tf_op jit(solution)/shard_map/while/body/eval_jaxpr/cond/branch_1_fun/grqk,kgpd->grpqd/dot_general | solution.py:73
  223.5 2.7 multiply_add_fusion
  229.5 51.1 %conditional.2 = ((f32[2,16,128]{2,1,0:T(8,128)S(1)}, f32[2,16,128]{2,1,0:T(8,128)S(1)}, f32[2,16,128,128]{3,2,1,0:T(8,128)}, f32[2,16,4,128,128]{4,3,2,1,0:T(8,128)}, f32[2,16,4,128]{3,2,1,0:T(4,128)S(1)})) conditional(s32[]{:T(128)} %convert_element_type.33, (f32[2,16,128]{2,1,0:T(8,128)S(1)}, f32[2,16,128]{2,1,0:T(8,128)S(1)}, ...), branch_computations={%region_5.5_spmd, %region_6.9_spmd} | conditional | flops 4875935744 | bytes 138629216 | solution.py:83
  229.6 1.6 fusion.3
  231.3 3.3 broadcast_multiply_fusion
  234.6 9.1 %fusion.7 = f32[2,256,4,16,128]{4,1,2,3,0:T(8,128)} fusion(bf16[2,16,128,128]{3,2,1,0:T(8,128)(2,1)S(1)} %get-tuple-element.183, bf16[4,256,2,4,128]{4,1,3,2,0:T(8,128)(2,1)} %get-tuple-element.189, s32[]{:T(128)} %get-tuple-element.182), kind=kOutput, calls=%fused_computation.13 | convolution fusion | flops 1073741824 | bytes 18350592 | tf_op jit(solution)/shard_map/while/body/eval_jaxpr/cond/branch_1_fun/grqd,kgpd->grpqk/dot_general | solution.py:57
  243.7 13.2 %fusion.40 = (f32[2,16,4,128]{3,2,1,0:T(4,128)S(1)}, bf16[2,16,4,128,256]{3,4,2,1,0:T(8,128)(2,1)}) fusion(f32[2,16,128,256]{2,3,1,0:T(8,128)} %get-tuple-element.327, f32[2,256,4,16,128]{4,1,2,3,0:T(8,128)} %fusion.7, bf16[2,16,4,128,128]{4,3,2,1,0:T(8,128)(2,1)} %get-tuple-element.188, bf16[4,256,2,128]{3,1,2,0:T(8,128)(2,1)} %get-tuple-element.181, ...), kind=kOutput, calls=%fused_computation.70 | convolution fusion | flops 1090502656 | bytes 33751552 | tf_op jit(solution)/shard_map/while/body/eval_jaxpr/cond/branch_1_fun/grpqd,kgd->grpqk/dot_general | solution.py:54
  257.0 10.0 %fusion.1 = f32[2,16,4,128,128]{4,3,2,1,0:T(8,128)} fusion(bf16[2,16,4,128,256]{3,4,2,1,0:T(8,128)(2,1)} %get-tuple-element.332, bf16[4,256,2,128]{3,1,2,0:T(8,128)(2,1)} %get-tuple-element.186, s32[]{:T(128)} %get-tuple-element.182), kind=kOutput, calls=%fused_computation.3 | convolution fusion | flops 1073741824 | bytes 16908800 | tf_op jit(solution)/shard_map/while/body/eval_jaxpr/cond/branch_1_fun/grpqk,kgd->grpqd/dot_general | solution.py:67
  267.0 9.5 %bitcast_add_fusion.1 = f32[2,16,4,128,128]{4,3,2,1,0:T(8,128)} fusion(f32[2,16,4,128,128]{4,3,2,1,0:T(8,128)} %fusion.1, f32[2,16,4,128,128]{4,3,2,1,0:T(8,128)} %get-tuple-element.187, f32[2,16,128]{2,1,0:T(8,128)S(1)} %get-tuple-element.320, bf16[4,256,2,4,128]{4,1,3,2,0:T(8,128)(2,1)S(1)} %get-tuple-element.190, s32[]{:T(128)} %get-tuple-element.182, ...), kind=kOutput, calls=%fused_computation.2 | convolution fusion | flops 1085276160 | bytes 29949956 | tf_op jit(solution)/shard_map/while/body/eval_jaxpr/cond/branch_1_fun/grqk,kgpd->grpqd/dot_general | solution.py:73
  276.6 2.7 multiply_add_fusion
  282.6 51.1 %conditional.2 = ((f32[2,16,128]{2,1,0:T(8,128)S(1)}, f32[2,16,128]{2,1,0:T(8,128)S(1)}, f32[2,16,128,128]{3,2,1,0:T(8,128)}, f32[2,16,4,128,128]{4,3,2,1,0:T(8,128)}, f32[2,16,4,128]{3,2,1,0:T(4,128)S(1)})) conditional(s32[]{:T(128)} %convert_element_type.33, (f32[2,16,128]{2,1,0:T(8,128)S(1)}, f32[2,16,128]{2,1,0:T(8,128)S(1)}, ...), branch_computations={%region_5.5_spmd, %region_6.9_spmd} | conditional | flops 4875935744 | bytes 138629216 | solution.py:83
  282.7 1.6 fusion.3
  284.4 3.3 broadcast_multiply_fusion
  287.7 9.1 %fusion.7 = f32[2,256,4,16,128]{4,1,2,3,0:T(8,128)} fusion(bf16[2,16,128,128]{3,2,1,0:T(8,128)(2,1)S(1)} %get-tuple-element.183, bf16[4,256,2,4,128]{4,1,3,2,0:T(8,128)(2,1)} %get-tuple-element.189, s32[]{:T(128)} %get-tuple-element.182), kind=kOutput, calls=%fused_computation.13 | convolution fusion | flops 1073741824 | bytes 18350592 | tf_op jit(solution)/shard_map/while/body/eval_jaxpr/cond/branch_1_fun/grqd,kgpd->grpqk/dot_general | solution.py:57
  296.8 13.2 %fusion.40 = (f32[2,16,4,128]{3,2,1,0:T(4,128)S(1)}, bf16[2,16,4,128,256]{3,4,2,1,0:T(8,128)(2,1)}) fusion(f32[2,16,128,256]{2,3,1,0:T(8,128)} %get-tuple-element.327, f32[2,256,4,16,128]{4,1,2,3,0:T(8,128)} %fusion.7, bf16[2,16,4,128,128]{4,3,2,1,0:T(8,128)(2,1)} %get-tuple-element.188, bf16[4,256,2,128]{3,1,2,0:T(8,128)(2,1)} %get-tuple-element.181, ...), kind=kOutput, calls=%fused_computation.70 | convolution fusion | flops 1090502656 | bytes 33751552 | tf_op jit(solution)/shard_map/while/body/eval_jaxpr/cond/branch_1_fun/grpqd,kgd->grpqk/dot_general | solution.py:54
  310.1 10.0 %fusion.1 = f32[2,16,4,128,128]{4,3,2,1,0:T(8,128)} fusion(bf16[2,16,4,128,256]{3,4,2,1,0:T(8,128)(2,1)} %get-tuple-element.332, bf16[4,256,2,128]{3,1,2,0:T(8,128)(2,1)} %get-tuple-element.186, s32[]{:T(128)} %get-tuple-element.182), kind=kOutput, calls=%fused_computation.3 | convolution fusion | flops 1073741824 | bytes 16908800 | tf_op jit(solution)/shard_map/while/body/eval_jaxpr/cond/branch_1_fun/grpqk,kgd->grpqd/dot_general | solution.py:67
  320.1 9.5 %bitcast_add_fusion.1 = f32[2,16,4,128,128]{4,3,2,1,0:T(8,128)} fusion(f32[2,16,4,128,128]{4,3,2,1,0:T(8,128)} %fusion.1, f32[2,16,4,128,128]{4,3,2,1,0:T(8,128)} %get-tuple-element.187, f32[2,16,128]{2,1,0:T(8,128)S(1)} %get-tuple-element.320, bf16[4,256,2,4,128]{4,1,3,2,0:T(8,128)(2,1)S(1)} %get-tuple-element.190, s32[]{:T(128)} %get-tuple-element.182, ...), kind=kOutput, calls=%fused_computation.2 | convolution fusion | flops 1085276160 | bytes 29949956 | tf_op jit(solution)/shard_map/while/body/eval_jaxpr/cond/branch_1_fun/grqk,kgpd->grpqd/dot_general | solution.py:73
  329.7 2.7 multiply_add_fusion
  333.8 2.0 convert_bitcast_fusion
  335.7 1.6 copy.92
  337.4 4.1 all-to-all-start.6
  341.5 5.6 %fusion.30 = bf16[128,2,16,4,128]{4,0,3,2,1:T(8,128)(2,1)S(1)} fusion(f32[2,16,4,128]{3,2,1,0:T(4,128)S(1)} %broadcast_divide_fusion.1, f32[2,16,128,128]{3,2,1,0:T(8,128)S(1)} %get-tuple-element.324, f32[2,16,4,128,128]{4,3,2,1,0:T(8,128)} %get-tuple-element.221, f32[2,16,128]{2,1,0:T(8,128)S(1)} %get-tuple-element.220), kind=kLoop, calls=%fused_computation.40 | loop fusion | flops 8388608 | bytes 14761984 | tf_op jit(solution)/shard_map/transpose | solution.py:124
  347.1 4.7 %copy.94 = bf16[128,2,16,4,128]{4,2,1,3,0:T(8,128)(2,1)} copy(bf16[128,2,16,4,128]{4,0,3,2,1:T(8,128)(2,1)S(1)} %fusion.30) | data formatting | bytes 8388608 | tf_op jit(solution)/shard_map/transpose | solution.py:124
  351.8 2.2 all-to-all-done.6
  354.0 5.4 %all-to-all-start.7 = ((bf16[128,32,4,128]{3,1,2,0:T(8,128)(2,1)}), bf16[128,32,4,128]{3,1,2,0:T(8,128)(2,1)}, u32[]{:S(2)}, u32[]{:S(2)}) async-start(bf16[128,32,4,128]{3,1,2,0:T(8,128)(2,1)} %bitcast.126), calls=%async_computation.7 | async-start | bytes 8388608 | tf_op jit(solution)/shard_map/all_to_all | solution.py:129
  360.5 45.2 %all-to-all-done.7 = bf16[128,32,4,128]{3,1,2,0:T(8,128)(2,1)} async-done(((bf16[128,32,4,128]{3,1,2,0:T(8,128)(2,1)}), bf16[128,32,4,128]{3,1,2,0:T(8,128)(2,1)}, u32[]{:S(2)}, u32[]{:S(2)}) %all-to-all-start.7) | async-done | bytes 4194336 | tf_op jit(solution)/shard_map/all_to_all | solution.py:129
  405.8 3.3 copy.95
  409.1 5.9 %copy.96 = bf16[32,128,4,128]{3,2,1,0:T(4,128)(2,1)} copy(bf16[32,128,4,128]{3,1,2,0:T(8,128)(2,1)S(1)} %bitcast.127) | data formatting | bytes 8388608
  (71 shorter events, 18.1 us)
Async XLA Ops:
  7.2 103.2 %all-gather.3.cloned.1.call-start = ((), (), s32[]{:S(2)}) async-start(), calls=%async_computation.8 | async-start | bytes 2359296 | tf_op jit(solution)/shard_map/all_gather | solution.py:100
  19.2 7.9 %all-to-all-start = ((bf16[32,8,128]{2,0,1:T(8,128)(2,1)}), bf16[32,8,128]{2,0,1:T(8,128)(2,1)S(1)}, u32[]{:S(2)}, u32[]{:S(2)}) async-start(bf16[32,8,128]{2,0,1:T(8,128)(2,1)} %copy.76), calls=%async_computation | async-start | bytes 131072 | tf_op jit(solution)/shard_map/all_to_all | solution.py:93
  27.1 8.1 %all-to-all-start.2 = ((bf16[32,8,128]{2,0,1:T(8,128)(2,1)}), bf16[32,8,128]{2,0,1:T(8,128)(2,1)S(1)}, u32[]{:S(2)}, u32[]{:S(2)}) async-start(bf16[32,8,128]{2,0,1:T(8,128)(2,1)} %copy.80), calls=%async_computation.2 | async-start | bytes 131072 | tf_op jit(solution)/shard_map/all_to_all | solution.py:95
  35.2 9.3 %all-to-all-start.5 = ((bf16[32,8,4,128]{3,0,2,1:T(8,128)(2,1)}), bf16[32,8,4,128]{3,0,2,1:T(8,128)(2,1)S(1)}, u32[]{:S(2)}, u32[]{:S(2)}) async-start(bf16[32,8,4,128]{3,0,2,1:T(8,128)(2,1)} %copy.86), calls=%async_computation.5 | async-start | bytes 524288 | tf_op jit(solution)/shard_map/all_to_all | solution.py:96
  44.5 13.2 %all-to-all-start.1 = ((bf16[32,128,128]{2,0,1:T(8,128)(2,1)}), bf16[32,128,128]{2,0,1:T(8,128)(2,1)S(1)}, u32[]{:S(2)}, u32[]{:S(2)}) async-start(bf16[32,128,128]{2,0,1:T(8,128)(2,1)} %copy.78), calls=%async_computation.1 | async-start | bytes 2097152 | tf_op jit(solution)/shard_map/all_to_all | solution.py:21
  48.7 64.8 %all-gather.5.cloned.1.call-start = ((), (), s32[]{:S(2)}) async-start(), calls=%async_computation.9 | async-start | bytes 2359296 | tf_op jit(solution)/shard_map/all_gather | solution.py:102
  56.1 7.1 %copy-start.2 = (s32[16]{0:T(128)S(1)}, s32[16]{0:T(128)}, u32[]{:S(2)}) copy-start(s32[16]{0:T(128)} %param.17) | copy-start | bytes 196
  57.7 47.3 %all-to-all-start.3 = ((bf16[32,128,4,128]{3,2,0,1:T(4,128)(2,1)}), bf16[32,128,4,128]{3,2,0,1:T(4,128)(2,1)}, u32[]{:S(2)}, u32[]{:S(2)}) async-start(bf16[32,128,4,128]{3,2,0,1:T(4,128)(2,1)} %copy.82), calls=%async_computation.3 | async-start | bytes 8388608 | tf_op jit(solution)/shard_map/all_to_all | solution.py:22
  160.8 9.6 %copy-start = (f32[2,16,128,128]{3,2,1,0:T(8,128)S(1)}, f32[2,16,128,128]{3,2,1,0:T(8,128)}, u32[]{:S(2)}) copy-start(f32[2,16,128,128]{3,2,1,0:T(8,128)} %get-tuple-element.185) | copy-start | bytes 6291460 | tf_op jit(solution)/shard_map/while/body/eval_jaxpr/cond
  173.1 1.3 copy-start.1
  213.9 9.6 %copy-start = (f32[2,16,128,128]{3,2,1,0:T(8,128)S(1)}, f32[2,16,128,128]{3,2,1,0:T(8,128)}, u32[]{:S(2)}) copy-start(f32[2,16,128,128]{3,2,1,0:T(8,128)} %get-tuple-element.185) | copy-start | bytes 6291460 | tf_op jit(solution)/shard_map/while/body/eval_jaxpr/cond
  226.2 1.3 copy-start.1
  267.0 9.6 %copy-start = (f32[2,16,128,128]{3,2,1,0:T(8,128)S(1)}, f32[2,16,128,128]{3,2,1,0:T(8,128)}, u32[]{:S(2)}) copy-start(f32[2,16,128,128]{3,2,1,0:T(8,128)} %get-tuple-element.185) | copy-start | bytes 6291460 | tf_op jit(solution)/shard_map/while/body/eval_jaxpr/cond
  279.3 1.3 copy-start.1
  320.1 9.6 %copy-start = (f32[2,16,128,128]{3,2,1,0:T(8,128)S(1)}, f32[2,16,128,128]{3,2,1,0:T(8,128)}, u32[]{:S(2)}) copy-start(f32[2,16,128,128]{3,2,1,0:T(8,128)} %get-tuple-element.185) | copy-start | bytes 6291460 | tf_op jit(solution)/shard_map/while/body/eval_jaxpr/cond
  332.4 1.3 copy-start.1
  337.4 16.6 %all-to-all-start.6 = ((bf16[128,32,128]{2,1,0:T(8,128)(2,1)}), bf16[128,32,128]{2,1,0:T(8,128)(2,1)S(1)}, u32[]{:S(2)}, u32[]{:S(2)}) async-start(bf16[128,32,128]{2,1,0:T(8,128)(2,1)} %bitcast.130), calls=%async_computation.6 | async-start | bytes 2097152 | tf_op jit(solution)/shard_map/all_to_all | solution.py:128
  354.0 51.8 %all-to-all-start.7 = ((bf16[128,32,4,128]{3,1,2,0:T(8,128)(2,1)}), bf16[128,32,4,128]{3,1,2,0:T(8,128)(2,1)}, u32[]{:S(2)}, u32[]{:S(2)}) async-start(bf16[128,32,4,128]{3,1,2,0:T(8,128)(2,1)} %bitcast.126), calls=%async_computation.7 | async-start | bytes 8388608 | tf_op jit(solution)/shard_map/all_to_all | solution.py:129
Sparse Core Ops, SparseCore 0:
  17.8 29.3 all-gather.2
  51.2 34.4 all-gather.4
where the time goes:
time: 426 us; the launch traced here: 422 us
  matrix products  185 us (43%)
  waiting for transfers between devices  60.8 us (14%)
  local copies, waits for them, and re-layouts  56.6 us (13%)
  blocking collectives  41.7 us (10%)
  starting transfers between devices  32.8 us (8%)
  other arithmetic  25.2 us (6%)
  between operations  14.2 us (3%)
  loops' own time  5.56 us (1%)
    dot_general x4, matrix products, update(): jnp.einsum('grpqd,kgd->grpqk', tangent_heads, key_block, preferred_elemen...  53 us
    all_to_all x1, waiting for transfers between devices, per_device(): lax.all_to_all(tangent_rows, 'uly', split_axis=0, concat_axis=1, tiled=True)  45.2 us
    dot_general x4, matrix products, update(): jnp.einsum('grpqk,kgd->grpqd', weighted.astype(jnp.bfloat16), value_block...  39.9 us
    dot_general x4, matrix products, update(): jnp.einsum('grqk,kgpd->grpqd', weights_half, value_tan, preferred_element...  38.2 us
    dot_general x4, matrix products, update(): jnp.einsum('grqd,kgpd->grpqk', query_heads, key_tan, preferred_element_ty...  36.5 us
    unnamed x9, local copies, waits for them, and re-layouts  21.1 us
    all_gather x1, blocking collectives, per_device(): key_piece = lax.all_gather(head_keys, 'blk', axis=0, tiled=True)  17.9 us
    all_gather x1, blocking collectives, per_device(): value_piece = lax.all_gather(head_values, 'blk', axis=0, tiled=True)  15.1 us
  transfers between devices with their start and end apart: 9, of which 7 were waited for; matrix products, arithmetic and copies ran while one was open for 9% of the time, Pallas kernels for 0%

commit v1 on v0

v1 whole, which is shorter than its diff:
```python
import functools

import jax
import jax.numpy as jnp
from jax import lax
from jax.experimental import pallas as pl
from jax.experimental.pallas import tpu as pltpu
from jax.sharding import PartitionSpec as P

TILE_SCORES = 256 * 1024


def positions(stored, span_order, span_rows):
    span_ids = stored // span_rows
    table_ids = jnp.arange(span_order.shape[0], dtype=jnp.int32)
    looked_up = jnp.sum(
        jnp.where(span_ids[:, None] == table_ids[None, :], span_order[None, :], 0), axis=1
    )
    return looked_up * span_rows + stored % span_rows


def exchange_and_attend(
    sizes, probes, group, packed, q_hbm, qt_hbm, bias_hbm, out_ref, tan_ref, *scratch
):
    gathered, q_ref, qt_ref, bias_ref, wide_in, wide_out, local_sem = scratch[:7]
    z_send, z_recv, one_send, one_recv, many_send, many_recv = scratch[7:]
    depth, side_y, side_x = sizes
    kv_heads = packed.shape[0]
    rows, _, head_size = q_ref.shape
    all_rows = rows * group
    keys_total = bias_ref.shape[1]
    tile = min(all_rows, TILE_SCORES // keys_total)
    scaling = head_size ** (-0.5)
    blk, uly = lax.axis_index("blk"), lax.axis_index("uly")
    z, c = blk // 2, blk % 2
    y, x = uly // side_x, uly % side_x

    def remote(src, dst, send, recv, target):
        return pltpu.make_async_remote_copy(
            src_ref=src,
            dst_ref=dst,
            send_sem=send,
            recv_sem=recv,
            device_id=target,
            device_id_type=pl.DeviceIdType.MESH,
        )

    def at_z(d):
        return (((z + d) % depth) * 2 + c, uly)

    def at_y(d):
        return (blk, ((y + d) % side_y) * side_x + x)

    at_x = (blk, y * side_x + (1 - x))
    at_core = (z * 2 + (1 - c), uly)

    def send_z(h):
        return [
            remote(
                packed.at[h],
                gathered.at[h, :, c, y, x, z],
                z_send.at[h, d - 1],
                z_recv.at[h, d - 1],
                at_z(d),
            )
            for d in range(1, depth)
        ]

    def to_x(h, which, block):
        return [remote(block, block, one_send.at[h, which], one_recv.at[h, which], at_x)]

    def to_y(h, which, block):
        return [
            remote(
                block,
                block,
                many_send.at[h, which, d - 1],
                many_recv.at[h, which, d - 1],
                at_y(d),
            )
            for d in range(1, side_y)
        ]

    def second(h):
        return to_x(h, 0, gathered.at[h, 0, c, y, x]) + to_y(h, 0, gathered.at[h, 1, c, y, x])

    def third(h):
        return to_y(h, 1, gathered.at[h, 0, c, y]) + to_x(h, 1, gathered.at[h, 1, c, :, x])

    def across_chip(h):
        block = gathered.at[h, :, c]
        return [remote(block, block, one_send.at[h, 2], one_recv.at[h, 2], at_core)]

    locals_in = [
        pltpu.make_async_copy(packed, gathered.at[:, :, c, y, x, z], local_sem.at[0]),
        pltpu.make_async_copy(q_hbm, q_ref, local_sem.at[1]),
        pltpu.make_async_copy(qt_hbm, qt_ref, local_sem.at[2]),
        pltpu.make_async_copy(bias_hbm, bias_ref, local_sem.at[3]),
    ]
    for copy in locals_in:
        copy.start()
    barrier = pltpu.get_barrier_semaphore()
    partners = [at_z(d) for d in range(1, depth)] + [at_y(d) for d in range(1, side_y)]
    partners += [at_x, at_core]
    for target in partners:
        pl.semaphore_signal(
            barrier, inc=1, device_id=target, device_id_type=pl.DeviceIdType.MESH
        )
    pl.semaphore_wait(barrier, len(partners))

    @pl.loop(0, kv_heads)
    def _(h):
        for copy in send_z(h):
            copy.start()

    for copy in locals_in:
        copy.wait()

    contract_last = (((1,), (1,)), ((), ()))

    def attend(h):
        def stream(half, index):
            return gathered[h, half, :, :, :, :, index].reshape(keys_total, head_size)

        q_rows = q_ref[:, pl.ds(pl.multiple_of(h * group, group), group), :]
        query = q_rows.reshape(all_rows, head_size)
        wide = group * probes
        qt_rows = qt_ref[:, pl.ds(pl.multiple_of(h * wide, wide), wide), :]
        wide_in[...] = qt_rows.reshape(all_rows * probes, head_size).astype(jnp.float32)
        key = stream(0, 0)
        value = stream(1, 0)
        value_all = jnp.concatenate([stream(1, p) for p in range(1 + probes)], axis=1)
        for start in range(0, all_rows, tile):
            q = query[start : start + tile]
            scores = lax.dot_general(q, key, contract_last, preferred_element_type=jnp.float32)
            scores = scores * scaling + bias_ref[start : start + tile, :]
            top = jnp.max(scores, axis=1, keepdims=True)
            weights = jnp.exp(scores - top)
            inverse = 1.0 / jnp.sum(weights, axis=1, keepdims=True)
            sums = jnp.dot(
                weights.astype(jnp.bfloat16), value_all, preferred_element_type=jnp.float32
            )
            primal = sums[:, :head_size] * inverse
            scaled = weights * scaling
            for p in range(probes):
                picked = pl.ds(start * probes + p, tile, stride=probes)
                left = jnp.concatenate([wide_in[picked, :].astype(jnp.bfloat16), q], axis=1)
                right = jnp.concatenate([key, stream(0, 1 + p)], axis=1)
                score_tan = lax.dot_general(
                    left, right, contract_last, preferred_element_type=jnp.float32
                )
                weighted = scaled * score_tan
                shift = jnp.sum(weighted, axis=1, keepdims=True)
                total = sums[:, head_size * (1 + p) : head_size * (2 + p)] + jnp.dot(
                    weighted.astype(jnp.bfloat16), value, preferred_element_type=jnp.float32
                )
                wide_out[picked, :] = (total - primal * shift) * inverse
            out_ref[
                start // group : (start + tile) // group,
                pl.ds(pl.multiple_of(h * group, group), group),
                :,
            ] = primal.astype(jnp.bfloat16).reshape(tile // group, group, head_size)
        tan_ref[:, pl.ds(pl.multiple_of(h * wide, wide), wide), :] = (
            wide_out[...].astype(jnp.bfloat16).reshape(rows, wide, head_size)
        )

    @pl.loop(0, kv_heads + 3)
    def _(t):
        @pl.when(t < kv_heads)
        def _():
            for copy in send_z(t):
                copy.wait_recv()
            for copy in second(t):
                copy.start()

        @pl.when((t >= 1) & (t < kv_heads + 1))
        def _():
            for copy in second(t - 1):
                copy.wait_recv()
            for copy in third(t - 1):
                copy.start()

        @pl.when((t >= 2) & (t < kv_heads + 2))
        def _():
            for copy in third(t - 2):
                copy.wait_recv()
            for copy in across_chip(t - 2):
                copy.start()

        @pl.when(t >= 3)
        def _():
            for copy in across_chip(t - 3):
                copy.wait_recv()
            attend(t - 3)

    @pl.loop(0, kv_heads)
    def _(h):
        for copy in send_z(h) + second(h) + third(h) + across_chip(h):
            copy.wait_send()


def per_device(queries, query_tangents, keys, key_tangents, values, value_tangents, span_order):
    rows, heads, head_size = queries.shape
    kv_heads = keys.shape[1]
    probes = key_tangents.shape[2]
    group = heads // kv_heads
    blks, ulys = lax.axis_size("blk"), lax.axis_size("uly")
    depth, side_x, side_y = blks // 2, 2, ulys // 2
    total_rows = rows * blks * ulys
    span_rows = total_rows // span_order.shape[0]
    tangents = query_tangents.reshape(rows, heads * probes, head_size)
    packed = jnp.stack(
        [
            jnp.concatenate(
                [
                    jnp.transpose(primal, (1, 0, 2))[:, None],
                    jnp.transpose(tangent, (1, 2, 0, 3)),
                ],
                axis=1,
            )
            for primal, tangent in ((keys, key_tangents), (values, value_tangents))
        ],
        axis=1,
    )
    me = lax.axis_index("blk") * ulys + lax.axis_index("uly")
    own = positions(me * rows + jnp.arange(rows, dtype=jnp.int32), span_order, span_rows)
    places = positions(jnp.arange(total_rows, dtype=jnp.int32), span_order, span_rows)
    places = jnp.transpose(
        places.reshape(depth, 2, side_y, side_x, rows), (1, 2, 3, 0, 4)
    ).reshape(total_rows)
    bias = jnp.where(places[None, :] <= own[:, None], 0.0, -1e30).astype(jnp.float32)
    bias = jnp.broadcast_to(bias[:, None], (rows, group, total_rows)).reshape(
        rows * group, total_rows
    )
    wide_rows = rows * group * probes
    pairs = rows * heads * total_rows
    dma = pltpu.SemaphoreType.DMA
    attention, tangent = pl.pallas_call(
        functools.partial(exchange_and_attend, (depth, side_y, side_x), probes, group),
        in_specs=[pl.BlockSpec(memory_space=pl.ANY)] * 4,
        out_specs=[pl.BlockSpec(memory_space=pltpu.VMEM)] * 2,
        out_shape=[
            jax.ShapeDtypeStruct(queries.shape, queries.dtype),
            jax.ShapeDtypeStruct(tangents.shape, tangents.dtype),
        ],
        scratch_shapes=[
            pltpu.VMEM(
                (kv_heads, 2, 2, side_y, side_x, depth, 1 + probes, rows, head_size),
                keys.dtype,
            ),
            pltpu.VMEM(queries.shape, queries.dtype),
            pltpu.VMEM(tangents.shape, tangents.dtype),
            pltpu.VMEM(bias.shape, bias.dtype),
            pltpu.VMEM((wide_rows, head_size), jnp.float32),
            pltpu.VMEM((wide_rows, head_size), jnp.float32),
            dma((4,)),
            dma((kv_heads, depth - 1)),
            dma((kv_heads, depth - 1)),
            dma((kv_heads, 3)),
            dma((kv_heads, 3)),
            dma((kv_heads, 2, side_y - 1)),
            dma((kv_heads, 2, side_y - 1)),
        ],
        cost_estimate=pl.CostEstimate(
            flops=2 * pairs * head_size * (2 + 4 * probes),
            transcendentals=pairs,
            bytes_accessed=packed.size * 2,
        ),
        compiler_params=pltpu.CompilerParams(
            collective_id=0, has_side_effects=True, vmem_limit_bytes=67043328
        ),
    )(packed, queries, tangents, bias)
    return attention, tangent.reshape(query_tangents.shape)


def solution(mesh):
    placed = (
        P(("blk", "uly"), None, None),
        P(("blk", "uly"), None, None, None),
        P(("blk", "uly"), None, None),
        P(("blk", "uly"), None, None, None),
        P(("blk", "uly"), None, None),
        P(("blk", "uly"), None, None, None),
        P(),
    )
    return jax.shard_map(
        per_device,
        mesh=mesh,
        in_specs=placed,
        out_specs=(P(("blk", "uly"), None, None), P(("blk", "uly"), None, None, None)),
        check_vma=False,
    )
```

time: 426 us -> 138 us (0.32)
  matrix products: 185 us -> 0 us
  Pallas kernels: 0 us -> 120 us
  waiting for transfers between devices: 60.8 us -> 0 us
  local copies, waits for them, and re-layouts: 56.6 us -> 14.6 us
  blocking collectives: 41.7 us -> 0 us
  starting transfers between devices: 32.8 us -> 0 us
  other arithmetic: 25.2 us -> 2.59 us
  between operations: 14.2 us -> 0.7 us
  loops' own time: 5.56 us -> 0 us
    dot_general x24 -> x0, matrix products: 185 us -> none  [the longest x4 53 us: update(): jnp.einsum('grpqd,kgd->grpqk', tangent_heads, key_block, preferred_elemen...]
    pallas_call x0 -> x1, Pallas kernels: none -> 120 us  [per_device(): pl.pallas_call(functools.partial(exchange_and_attend, (depth, side_y, sid...]
    all_to_all x7 -> x0, waiting for transfers between devices: 60.8 us -> none  [the longest x1 45.2 us: per_device(): lax.all_to_all(tangent_rows, 'uly', split_axis=0, concat_axis=1, tiled=True)]
    all_gather x2 -> x0, blocking collectives: 33.1 us -> none  [the longest x1 17.9 us: per_device(): key_piece = lax.all_gather(head_keys, 'blk', axis=0, tiled=True)]
    all_to_all x7 -> x0, starting transfers between devices: 32.8 us -> none  [the longest x1 5.47 us: per_device(): lax.all_to_all(query_tangents, 'uly', split_axis=1, concat_axis=0, tiled=...]
    mul x4 -> x0, other arithmetic: 13.3 us -> none  [update(): weighted = weights_full[:, :, None] * (score_tan * scaling)]
    all_to_all x8 -> x0, local copies, waits for them, and re-layouts: 11.4 us -> none  [the longest x1 5.36 us: per_device(): lax.all_to_all(query_tangents, 'uly', split_axis=1, concat_axis=0, tiled=...]
    all_to_all x1 -> x0, blocking collectives: 8.66 us -> none  [per_device(): lax.all_to_all(key_tangents, 'uly', split_axis=1, concat_axis=0, tiled=True)]
  transfers between devices with their start and end apart: 9 -> 0, of which waited for: 7 -> 0; matrix products, arithmetic and copies ran while one was open for 9% -> 0% of each run, Pallas kernels for 0% -> 0%
where the time goes in v1:
time: 138 us; the launch traced here: 137 us
  Pallas kernels  120 us (87%)
  local copies, waits for them, and re-layouts  14.6 us (11%)
  other arithmetic  2.59 us (2%)
    pallas_call x1, Pallas kernels, per_device(): pl.pallas_call(functools.partial(exchange_and_attend, (depth, side_y, sid...  120 us
    unnamed x6, local copies, waits for them, and re-layouts  12.8 us

profile of v1, /device:TPU:10, one launch (start us, length us, event | category | flops | bytes accessed | tf_op | source)
XLA Modules:
  0.0 137.4 jit_solution(16377579152472379729)
XLA Ops:
  0.7 0.7 select_reduce_fusion.1
  1.4 0.7 select_reduce_fusion
  2.2 0.1 mul.23
  2.3 0.1 le.19
  2.4 0.9 copy.34
  3.2 0.9 copy.33
  4.1 0.1 compare_select_fusion
  4.2 1.1 copy.32
  5.2 1.1 copy.31
  6.3 0.1 maximum_bitcast_fusion
  6.4 0.9 pad_maximum_fusion.packed
  7.3 1.6 %broadcast_in_dim.59 = f32[32,16,1024]{2,1,0:T(8,128)} broadcast(f32[32,1024]{1,0:T(8,128)S(1)} %compare_select_fusion), dimensions={0,2} | broadcast | bytes 2228224 | tf_op jit(solution)/shard_map/broadcast_in_dim | solution.py:232
  8.8 119.6 %shard_map.86 = (bf16[32,128,128]{2,1,0:T(8,128)(2,1)}, bf16[32,512,128]{2,1,0:T(8,128)(2,1)}) custom-call(bf16[8,2,5,32,128]{4,3,2,1,0:T(8,128)(2,1)} %pad_maximum_fusion.packed, bf16[32,128,128]{2,1,0:T(8,128)(2,1)} %q_hbm.1, bf16[32,512,128]{2,1,0:T(8,128)(2,1)} %bitcast.31, f32[512,1024]{1,0:T(8,128)} %bitcast.26), custom_call_target="tpu_custom_call" | custom-call | flops 19327352832 | bytes 655360 | tf_op jit(solution)/shard_map/pallas_call | solution.py:238
  128.4 2.3 %copy.37 = bf16[32,128,128]{2,1,0:T(8,128)(2,1)} copy(bf16[32,128,128]{2,1,0:T(8,128)(2,1)} %get-tuple-element.10) | data formatting | bytes 2097152
  130.7 6.7 %copy.38 = bf16[32,128,4,128]{3,2,1,0:T(4,128)(2,1)} copy(bf16[32,128,4,128]{3,2,1,0:T(4,128)(2,1)} %bitcast.25) | data formatting | bytes 8388608
  (6 shorter events, 0.1 us)

commit v2 on v1

v2 whole, which is shorter than its diff:
```python
import functools

import jax
import jax.numpy as jnp
import numpy as np
from jax import lax
from jax.experimental import pallas as pl
from jax.experimental.pallas import tpu as pltpu
from jax.sharding import PartitionSpec as P

TILE_SCORES = 256 * 1024
LAST = 2


def exchange_and_attend(
    sizes, probes, group, span_rows, order_ref, place_ref, packed, packed_last, q_hbm, qt_hbm,
    out_ref, tan_ref, *scratch
):
    pair, last, q_ref, qt_ref, places, bias_ref, wide_in, wide_out, local_sem = scratch[:9]
    z_send, z_recv, one_send, one_recv, many_send, many_recv = scratch[9:15]
    plane_send, plane_recv, step_send, step_recv = scratch[15:]
    depth, side_y, side_x = sizes
    kv_heads = packed.shape[0]
    rows, _, head_size = q_ref.shape
    all_rows = rows * group
    keys_total = bias_ref.shape[1]
    tile = min(all_rows, TILE_SCORES // keys_total)
    scaling = head_size ** (-0.5)
    blk, uly = lax.axis_index("blk"), lax.axis_index("uly")
    z, c = blk // 2, blk % 2
    y, x = uly // side_x, uly % side_x

    def remote(src, dst, send, recv, target):
        return pltpu.make_async_remote_copy(
            src_ref=src,
            dst_ref=dst,
            send_sem=send,
            recv_sem=recv,
            device_id=target,
            device_id_type=pl.DeviceIdType.MESH,
        )

    def at_z(d):
        return (((z + d) % depth) * 2 + c, uly)

    def at_plane(dy, dx):
        return (blk, ((y + dy) % side_y) * side_x + (x + dx) % side_x)

    at_core = (z * 2 + (1 - c), uly)
    offsets = [(dy, dx) for dy in range(side_y) for dx in range(side_x) if dy or dx]

    def send_z(h):
        return [
            remote(
                packed.at[h],
                pair.at[h, :, c, z, y, x],
                z_send.at[h, d - 1],
                z_recv.at[h, d - 1],
                at_z(d),
            )
            for d in range(1, depth)
        ]

    def to_x(h, which, block):
        return [
            remote(block, block, one_send.at[h, which], one_recv.at[h, which], at_plane(0, 1))
        ]

    def to_y(h, which, block):
        return [
            remote(
                block,
                block,
                many_send.at[h, which, d - 1],
                many_recv.at[h, which, d - 1],
                at_plane(d, 0),
            )
            for d in range(1, side_y)
        ]

    def second(h):
        return to_x(h, 0, pair.at[h, 0, c, :, y, x]) + to_y(h, 0, pair.at[h, 1, c, :, y, x])

    def third(h):
        return to_y(h, 1, pair.at[h, 0, c, :, y]) + to_x(h, 1, pair.at[h, 1, c, :, :, x])

    def across_chip(h):
        return [
            remote(block, block, one_send.at[h, which], one_recv.at[h, which], at_core)
            for which, block in ((2, pair.at[h, :, c]), (3, last.at[h, c]))
        ]

    planes = [
        remote(
            packed_last, last.at[:, c, z, y, x], plane_send.at[n], plane_recv.at[n], at_plane(*d)
        )
        for n, d in enumerate(offsets)
    ]

    def each_step(h, s, act):
        for way, sign in enumerate((1, -1)):
            origin = z - sign * (s - 1)
            block = last.at[h, c, jnp.clip(origin, 0, depth - 1)]
            target = jnp.clip(z + sign, 0, depth - 1)
            copy = remote(
                block,
                block,
                step_send.at[h, s - 1, way],
                step_recv.at[h, s - 1, way],
                (target * 2 + c, uly),
            )
            arrives = z - sign * s
            sends = (origin >= 0) & (origin < depth) & (z + sign >= 0) & (z + sign < depth)
            gets = (arrives >= 0) & (arrives < depth)

            @pl.when(gets if act == "wait_recv" else sends)
            def _(copy=copy):
                getattr(copy, act)()

    locals_in = [
        pltpu.make_async_copy(packed, pair.at[:, :, c, z, y, x], local_sem.at[0]),
        pltpu.make_async_copy(packed_last, last.at[:, c, z, y, x], local_sem.at[1]),
        pltpu.make_async_copy(place_ref, places, local_sem.at[2]),
        pltpu.make_async_copy(q_hbm, q_ref, local_sem.at[3]),
        pltpu.make_async_copy(qt_hbm, qt_ref, local_sem.at[4]),
    ]
    barrier = pltpu.get_barrier_semaphore()
    partners = [at_z(d) for d in range(1, depth)] + [at_plane(*d) for d in offsets] + [at_core]
    for target in partners:
        pl.semaphore_signal(
            barrier, inc=1, device_id=target, device_id_type=pl.DeviceIdType.MESH
        )
    for copy in locals_in:
        copy.start()
    pl.semaphore_wait(barrier, len(partners))
    for copy in send_z(0) + planes + send_z(1):
        copy.start()
    for copy in locals_in:
        copy.wait()

    spans = order_ref.shape[0]
    looked_up = jnp.zeros((1, keys_total), jnp.int32)
    for span in range(spans):
        looked_up = jnp.where(places[0:1, :] == span, order_ref[span], looked_up)
    key_places = looked_up * span_rows + places[1:2, :]
    first = (blk * (side_y * side_x) + uly) * rows
    base = order_ref[first // span_rows] * span_rows + first % span_rows
    row = lax.broadcasted_iota(jnp.int32, (all_rows, 1), 0)
    row = base + lax.shift_right_logical(row, jnp.full_like(row, group.bit_length() - 1))
    bias_ref[...] = jnp.where(key_places <= row, 0.0, -1e30).astype(jnp.float32)

    for copy in planes:
        copy.wait_recv()

    contract_last = (((1,), (1,)), ((), ()))

    def attend(h):
        def stream(index):
            half = pair.shape[6]
            if index < 2 * half:
                found = pair[h, index // half, :, :, :, :, index % half]
            else:
                found = last[h, :, :, :, :, index - 2 * half]
            return found.reshape(keys_total, head_size)

        q_rows = q_ref[:, pl.ds(pl.multiple_of(h * group, group), group), :]
        query = q_rows.reshape(all_rows, head_size)
        wide = group * probes
        qt_rows = qt_ref[:, pl.ds(pl.multiple_of(h * wide, wide), wide), :]
        wide_in[...] = qt_rows.reshape(all_rows * probes, head_size).astype(jnp.float32)
        key = stream(0)
        value = stream(1 + probes)
        value_all = jnp.concatenate([stream(1 + probes + p) for p in range(1 + probes)], axis=1)
        for start in range(0, all_rows, tile):
            q = query[start : start + tile]
            scores = lax.dot_general(q, key, contract_last, preferred_element_type=jnp.float32)
            scores = scores * scaling + bias_ref[start : start + tile, :]
            top = jnp.max(scores, axis=1, keepdims=True)
            weights = jnp.exp(scores - top)
            inverse = 1.0 / jnp.sum(weights, axis=1, keepdims=True)
            sums = jnp.dot(
                weights.astype(jnp.bfloat16), value_all, preferred_element_type=jnp.float32
            )
            primal = sums[:, :head_size] * inverse
            scaled = weights * scaling
            for p in range(probes):
                picked = pl.ds(start * probes + p, tile, stride=probes)
                left = jnp.concatenate([wide_in[picked, :].astype(jnp.bfloat16), q], axis=1)
                right = jnp.concatenate([key, stream(1 + p)], axis=1)
                score_tan = lax.dot_general(
                    left, right, contract_last, preferred_element_type=jnp.float32
                )
                weighted = scaled * score_tan
                shift = jnp.sum(weighted, axis=1, keepdims=True)
                total = sums[:, head_size * (1 + p) : head_size * (2 + p)] + jnp.dot(
                    weighted.astype(jnp.bfloat16), value, preferred_element_type=jnp.float32
                )
                wide_out[picked, :] = (total - primal * shift) * inverse
            out_ref[
                start // group : (start + tile) // group,
                pl.ds(pl.multiple_of(h * group, group), group),
                :,
            ] = primal.astype(jnp.bfloat16).reshape(tile // group, group, head_size)
        tan_ref[:, pl.ds(pl.multiple_of(h * wide, wide), wide), :] = (
            wide_out[...].astype(jnp.bfloat16).reshape(rows, wide, head_size)
        )

    steps = range(1, depth)

    @pl.loop(min(0, 3 - depth), kv_heads + 3)
    def _(t):
        @pl.when((t >= 0) & (t < kv_heads - 2))
        def _():
            for copy in send_z(t + 2):
                copy.start()

        @pl.when((t >= 0) & (t < kv_heads))
        def _():
            for copy in send_z(t):
                copy.wait_recv()
            for copy in second(t):
                copy.start()

        for s in steps:
            h = t - s + depth - 2

            @pl.when((h >= 0) & (h < kv_heads))
            def _(h=h, s=s):
                if s > 1:
                    each_step(h, s - 1, "wait_recv")
                each_step(h, s, "start")

        @pl.when((t == 0) | ((t >= 2) & (t < kv_heads + 1)))
        def _():
            h = jnp.maximum(t - 1, 0)
            for copy in second(h):
                copy.wait_recv()
            for copy in third(h):
                copy.start()

        @pl.when((t >= 2) & (t < kv_heads + 2))
        def _():
            for copy in third(t - 2):
                copy.wait_recv()
            each_step(t - 2, depth - 1, "wait_recv")
            for copy in across_chip(t - 2):
                copy.start()

        @pl.when(t >= 3)
        def _():
            for copy in across_chip(t - 3):
                copy.wait_recv()
            attend(t - 3)

    for copy in planes:
        copy.wait_send()

    @pl.loop(0, kv_heads)
    def _(h):
        for copy in send_z(h) + second(h) + third(h) + across_chip(h):
            copy.wait_send()
        for s in steps:
            each_step(h, s, "wait_send")


def per_device(queries, query_tangents, keys, key_tangents, values, value_tangents, span_order):
    rows, heads, head_size = queries.shape
    kv_heads = keys.shape[1]
    probes = key_tangents.shape[2]
    group = heads // kv_heads
    blks, ulys = lax.axis_size("blk"), lax.axis_size("uly")
    depth, side_x, side_y = blks // 2, 2, ulys // 2
    total_rows = rows * blks * ulys
    span_rows = total_rows // span_order.shape[0]
    tangents = query_tangents.reshape(rows, heads * probes, head_size)
    streams = jnp.concatenate(
        [
            jnp.transpose(keys, (1, 0, 2))[:, None],
            jnp.transpose(key_tangents, (1, 2, 0, 3)),
            jnp.transpose(values, (1, 0, 2))[:, None],
            jnp.transpose(value_tangents, (1, 2, 0, 3)),
        ],
        axis=1,
    )
    half = (streams.shape[1] - LAST) // 2
    packed = streams[:, : 2 * half].reshape(kv_heads, 2, half, rows, head_size)
    packed_last = streams[:, 2 * half :]
    stored = np.arange(total_rows).reshape(depth, 2, ulys, rows)
    stored = stored.transpose(1, 0, 2, 3).reshape(total_rows)
    place_table = np.stack([stored // span_rows, stored % span_rows]).astype(np.int32)
    wide_rows = rows * group * probes
    pairs = rows * heads * total_rows
    dma = pltpu.SemaphoreType.DMA
    attention, tangent = pl.pallas_call(
        functools.partial(
            exchange_and_attend, (depth, side_y, side_x), probes, group, span_rows
        ),
        in_specs=[pl.BlockSpec(memory_space=pltpu.SMEM)]
        + [pl.BlockSpec(memory_space=pl.ANY)] * 5,
        out_specs=[pl.BlockSpec(memory_space=pltpu.VMEM)] * 2,
        out_shape=[
            jax.ShapeDtypeStruct(queries.shape, queries.dtype),
            jax.ShapeDtypeStruct(tangents.shape, tangents.dtype),
        ],
        scratch_shapes=[
            pltpu.VMEM(
                (kv_heads, 2, 2, depth, side_y, side_x, half, rows, head_size), keys.dtype
            ),
            pltpu.VMEM(
                (kv_heads, 2, depth, side_y, side_x, streams.shape[1] - 2 * half, rows, head_size),
                keys.dtype,
            ),
            pltpu.VMEM(queries.shape, queries.dtype),
            pltpu.VMEM(tangents.shape, tangents.dtype),
            pltpu.VMEM(place_table.shape, jnp.int32),
            pltpu.VMEM((rows * group, total_rows), jnp.float32),
            pltpu.VMEM((wide_rows, head_size), jnp.float32),
            pltpu.VMEM((wide_rows, head_size), jnp.float32),
            dma((5,)),
            dma((kv_heads, depth - 1)),
            dma((kv_heads, depth - 1)),
            dma((kv_heads, 4)),
            dma((kv_heads, 4)),
            dma((kv_heads, 2, side_y - 1)),
            dma((kv_heads, 2, side_y - 1)),
            dma((side_y * side_x - 1,)),
            dma((side_y * side_x - 1,)),
            dma((kv_heads, depth - 1, 2)),
            dma((kv_heads, depth - 1, 2)),
        ],
        cost_estimate=pl.CostEstimate(
            flops=2 * pairs * head_size * (2 + 4 * probes),
            transcendentals=pairs,
            bytes_accessed=packed.size * 2,
        ),
        compiler_params=pltpu.CompilerParams(
            collective_id=0, has_side_effects=True, vmem_limit_bytes=67043328
        ),
    )(span_order, place_table, packed, packed_last, queries, tangents)
    return attention, tangent.reshape(query_tangents.shape)


def solution(mesh):
    placed = (
        P(("blk", "uly"), None, None),
        P(("blk", "uly"), None, None, None),
        P(("blk", "uly"), None, None),
        P(("blk", "uly"), None, None, None),
        P(("blk", "uly"), None, None),
        P(("blk", "uly"), None, None, None),
        P(),
    )
    return jax.shard_map(
        per_device,
        mesh=mesh,
        in_specs=placed,
        out_specs=(P(("blk", "uly"), None, None), P(("blk", "uly"), None, None, None)),
        check_vma=False,
    )
```

time: 138 us -> 121 us (0.88)
  Pallas kernels: 120 us -> 107 us
  local copies, waits for them, and re-layouts: 14.6 us -> 11.8 us
  other arithmetic: 2.59 us -> 0.86 us
    pallas_call x1, Pallas kernels: 120 us -> 107 us  [per_device(): pl.pallas_call(functools.partial(exchange_and_attend, (depth, side_y, sid...]
    unnamed x6 -> x2, local copies, waits for them, and re-layouts: 12.8 us -> 9 us
    reduce_sum x2 -> x0, other arithmetic: 1.48 us -> none  [positions(): jnp.sum(jnp.where(span_ids[:, None] == table_ids[None, :], span_order[Non...]
where the time goes in v2:
time: 121 us; the launch traced here: 120 us
  Pallas kernels  107 us (88%)
  local copies, waits for them, and re-layouts  11.8 us (10%)
    pallas_call x1, Pallas kernels, per_device(): pl.pallas_call(functools.partial(exchange_and_attend, (depth, side_y, sid...  107 us
    unnamed x2, local copies, waits for them, and re-layouts  9 us

profile of v2, /device:TPU:10, one launch (start us, length us, event | category | flops | bytes accessed | tf_op | source)
XLA Modules:
  0.0 120.4 jit_solution(4651407888689378428)
XLA Ops:
  0.6 0.9 copy_bitcast_fusion.2
  1.5 1.2 %copy_bitcast_fusion = (bf16[8,4,32,128]{3,2,1,0:T(8,128)(2,1)S(1)}, bf16[8,4,32,128]{3,2,1,0:T(8,128)(2,1)S(1)}) fusion(bf16[32,8,4,128]{3,2,1,0:T(4,128)(2,1)} %param.13, bf16[32,8,4,128]{3,2,1,0:T(4,128)(2,1)} %param.11), kind=kLoop, calls=%fused_computation.3 | loop fusion | bytes 1048576 | tf_op jit(solution)/shard_map/transpose | solution.py:281
  2.8 0.9 pad_maximum_fusion
  3.6 0.7 slice.8.packed_last
  4.3 107.1 %shard_map.95 = (bf16[32,128,128]{2,1,0:T(8,128)(2,1)}, bf16[32,512,128]{2,1,0:T(8,128)(2,1)}) custom-call(s32[16]{0:T(128)} %order_ref.1, s32[2,1024]{1,0:T(2,128)} %constant.2.clone.place_ref, bf16[8,2,4,32,128]{4,3,2,1,0:T(8,128)(2,1)} %bitcast.16, bf16[8,2,32,128]{3,2,1,0:T(8,128)(2,1)} %slice.8.packed_last, bf16[32,128,128]{2,1,0:T(8,128)(2,1)} %q_hbm.1, ...), custom_call_target="tpu_custom_call" | custom-call | flops 19327352832 | bytes 524288 | tf_op jit(solution)/shard_map/pallas_call | solution.py:294
  111.4 2.3 %copy.20 = bf16[32,128,128]{2,1,0:T(8,128)(2,1)} copy(bf16[32,128,128]{2,1,0:T(8,128)(2,1)} %get-tuple-element.12) | data formatting | bytes 2097152
  113.7 6.7 %copy.21 = bf16[32,128,4,128]{3,2,1,0:T(4,128)(2,1)} copy(bf16[32,128,4,128]{3,2,1,0:T(4,128)(2,1)} %bitcast.15) | data formatting | bytes 8388608

commit v3 on v2

--- a/solution.py
+++ b/solution.py
@@ -14,11 +14,11 @@
 
 def exchange_and_attend(
     sizes, probes, group, span_rows, order_ref, place_ref, packed, packed_last, q_hbm, qt_hbm,
-    out_ref, tan_ref, *scratch
+    out_hbm, tan_hbm, *scratch
 ):
     pair, last, q_ref, qt_ref, places, bias_ref, wide_in, wide_out, local_sem = scratch[:9]
     z_send, z_recv, one_send, one_recv, many_send, many_recv = scratch[9:15]
-    plane_send, plane_recv, step_send, step_recv = scratch[15:]
+    plane_send, plane_recv, step_send, step_recv, out_ref, tan_ref, out_sem = scratch[15:]
     depth, side_y, side_x = sizes
     kv_heads = packed.shape[0]
     rows, _, head_size = q_ref.shape
@@ -205,30 +205,29 @@
             wide_out[...].astype(jnp.bfloat16).reshape(rows, wide, head_size)
         )
 
+    def put_out(h):
+        wide = group * probes
+        narrow_part = pl.ds(pl.multiple_of(h * group, group), group)
+        wide_part = pl.ds(pl.multiple_of(h * wide, wide), wide)
+        return [
+            pltpu.make_async_copy(
+                out_ref.at[:, narrow_part], out_hbm.at[:, narrow_part], out_sem.at[h, 0]
+            ),
+            pltpu.make_async_copy(
+                tan_ref.at[:, wide_part], tan_hbm.at[:, wide_part], out_sem.at[h, 1]
+            ),
+        ]
+
     steps = range(1, depth)
 
     @pl.loop(min(0, 3 - depth), kv_heads + 3)
     def _(t):
-        @pl.when((t >= 0) & (t < kv_heads - 2))
-        def _():
-            for copy in send_z(t + 2):
-                copy.start()
-
         @pl.when((t >= 0) & (t < kv_heads))
         def _():
             for copy in send_z(t):
                 copy.wait_recv()
             for copy in second(t):
                 copy.start()
-
-        for s in steps:
-            h = t - s + depth - 2
-
-            @pl.when((h >= 0) & (h < kv_heads))
-            def _(h=h, s=s):
-                if s > 1:
-                    each_step(h, s - 1, "wait_recv")
-                each_step(h, s, "start")
 
         @pl.when((t == 0) | ((t >= 2) & (t < kv_heads + 1)))
         def _():
@@ -238,6 +237,20 @@
             for copy in third(h):
                 copy.start()
 
+        for s in steps:
+            h = t - s + depth - 2
+
+            @pl.when((h >= 0) & (h < kv_heads))
+            def _(h=h, s=s):
+                if s > 1:
+                    each_step(h, s - 1, "wait_recv")
+                each_step(h, s, "start")
+
+        @pl.when((t >= 0) & (t < kv_heads - 2))
+        def _():
+            for copy in send_z(t + 2):
+                copy.start()
+
         @pl.when((t >= 2) & (t < kv_heads + 2))
         def _():
             for copy in third(t - 2):
@@ -251,6 +264,8 @@
             for copy in across_chip(t - 3):
                 copy.wait_recv()
             attend(t - 3)
+            for copy in put_out(t - 3):
+                copy.start()
 
     for copy in planes:
         copy.wait_send()
@@ -261,6 +276,45 @@
             copy.wait_send()
         for s in steps:
             each_step(h, s, "wait_send")
+        for copy in put_out(h):
+            copy.wait()
+
+
+def settle(parts, *refs):
+    count = len(refs) // 4
+    sources, targets, held, sems = (refs[n * count : (n + 1) * count] for n in range(4))
+
+    def pieces(sources, targets, side):
+        return [
+            pltpu.make_async_copy(
+                source.at[n * (source.shape[0] // parts) : (n + 1) * (source.shape[0] // parts)],
+                target.at[n * (source.shape[0] // parts) : (n + 1) * (source.shape[0] // parts)],
+                sem.at[side, n],
+            )
+            for n in range(parts)
+            for source, target, sem in zip(sources, targets, sems)
+        ]
+
+    loads, stores = pieces(sources, held, 0), pieces(held, targets, 1)
+    for copy in loads:
+        copy.start()
+    for load, store in zip(loads, stores):
+        load.wait()
+        store.start()
+    for copy in stores:
+        copy.wait()
+
+
+def settled(arrays):
+    parts = min(8, arrays[0].shape[0])
+    return pl.pallas_call(
+        functools.partial(settle, parts),
+        in_specs=[pl.BlockSpec(memory_space=pl.ANY)] * len(arrays),
+        out_specs=[pl.BlockSpec(memory_space=pl.ANY)] * len(arrays),
+        out_shape=[jax.ShapeDtypeStruct(a.shape, a.dtype) for a in arrays],
+        scratch_shapes=[pltpu.VMEM(a.shape, a.dtype) for a in arrays]
+        + [pltpu.SemaphoreType.DMA((2, parts))] * len(arrays),
+    )(*arrays)
 
 
 def per_device(queries, query_tangents, keys, key_tangents, values, value_tangents, span_order):
@@ -297,7 +351,7 @@
         ),
         in_specs=[pl.BlockSpec(memory_space=pltpu.SMEM)]
         + [pl.BlockSpec(memory_space=pl.ANY)] * 5,
-        out_specs=[pl.BlockSpec(memory_space=pltpu.VMEM)] * 2,
+        out_specs=[pl.BlockSpec(memory_space=pl.ANY)] * 2,
         out_shape=[
             jax.ShapeDtypeStruct(queries.shape, queries.dtype),
             jax.ShapeDtypeStruct(tangents.shape, tangents.dtype),
@@ -327,6 +381,9 @@
             dma((side_y * side_x - 1,)),
             dma((kv_heads, depth - 1, 2)),
             dma((kv_heads, depth - 1, 2)),
+            pltpu.VMEM(queries.shape, queries.dtype),
+            pltpu.VMEM(tangents.shape, tangents.dtype),
+            dma((kv_heads, 2)),
         ],
         cost_estimate=pl.CostEstimate(
             flops=2 * pairs * head_size * (2 + 4 * probes),
@@ -337,6 +394,7 @@
             collective_id=0, has_side_effects=True, vmem_limit_bytes=67043328
         ),
     )(span_order, place_table, packed, packed_last, queries, tangents)
+    attention, tangent = settled([attention, tangent])
     return attention, tangent.reshape(query_tangents.shape)
 
 

time: 121 us -> 110 us (0.909)
  local copies, waits for them, and re-layouts: 11.8 us -> 2.79 us
  Pallas kernels: 107 us -> 105 us
    unnamed x2 -> x0, local copies, waits for them, and re-layouts: 9 us -> none
    pallas_call x1, Pallas kernels: 107 us -> 100 us  [per_device(): pl.pallas_call(functools.partial(exchange_and_attend, (depth, side_y, sid...]
    pallas_call x0 -> x1, Pallas kernels: none -> 4.9 us  [settled(): pl.pallas_call(functools.partial(settle, parts), in_specs=[pl.BlockSpec(m...]
where the time goes in v3:
time: 110 us; the launch traced here: 109 us
  Pallas kernels  105 us (95%)
  local copies, waits for them, and re-layouts  2.79 us (3%)
    pallas_call x1, Pallas kernels, per_device(): pl.pallas_call(functools.partial(exchange_and_attend, (depth, side_y, sid...  100 us
    pallas_call x1, Pallas kernels, settled(): pl.pallas_call(functools.partial(settle, parts), in_specs=[pl.BlockSpec(m...  4.9 us

profile of v3, /device:TPU:10, one launch (start us, length us, event | category | flops | bytes accessed | tf_op | source)
XLA Modules:
  0.0 109.4 jit_solution(13148739348055026886)
XLA Ops:
  0.6 0.9 copy_bitcast_fusion.2
  1.5 1.2 %copy_bitcast_fusion = (bf16[8,4,32,128]{3,2,1,0:T(8,128)(2,1)S(1)}, bf16[8,4,32,128]{3,2,1,0:T(8,128)(2,1)S(1)}) fusion(bf16[32,8,4,128]{3,2,1,0:T(4,128)(2,1)} %param.13, bf16[32,8,4,128]{3,2,1,0:T(4,128)(2,1)} %param.11), kind=kLoop, calls=%fused_computation.3 | loop fusion | bytes 1048576 | tf_op jit(solution)/shard_map/transpose | solution.py:335
  2.8 0.9 pad_maximum_fusion
  3.6 0.7 slice.8.packed_last
  4.3 100.2 %shard_map.95 = (bf16[32,128,128]{2,1,0:T(8,128)(2,1)}, bf16[32,512,128]{2,1,0:T(8,128)(2,1)}) custom-call(s32[16]{0:T(128)} %order_ref.1, s32[2,1024]{1,0:T(2,128)} %constant.2.clone.place_ref, bf16[8,2,4,32,128]{4,3,2,1,0:T(8,128)(2,1)} %bitcast.15, bf16[8,2,32,128]{3,2,1,0:T(8,128)(2,1)} %slice.8.packed_last, bf16[32,128,128]{2,1,0:T(8,128)(2,1)} %q_hbm.1, ...), custom_call_target="tpu_custom_call" | custom-call | flops 19327352832 | bytes 524288 | tf_op jit(solution)/shard_map/pallas_call | solution.py:348
  104.5 4.9 %shard_map.96 = (bf16[32,128,128]{2,1,0:T(8,128)(2,1)}, bf16[32,512,128]{2,1,0:T(8,128)(2,1)}) custom-call(bf16[32,128,128]{2,1,0:T(8,128)(2,1)} %get-tuple-element.6.refs_0_, bf16[32,512,128]{2,1,0:T(8,128)(2,1)} %get-tuple-element.7.refs_1_), custom_call_target="tpu_custom_call" | custom-call | tf_op jit(solution)/shard_map/pallas_call | solution.py:310
